TPU v7x, 32 devices: a whole 2x2x4 slice. The times are simulated.
32 devices in a mesh: gz: 4 (over y, x), gy: 8 (over z, core).
Axes of the slice: x: 2, y: 2, z: 4, core: 2. Of those that a mesh axis runs over, the one named last changes fastest.
Arguments:
- fixed: float32 [128, 512, 256], P('gz', 'gy'), may hold values from -6 to 6
- moving: float32 [128, 512, 256], P('gz', 'gy'), may hold values from -6 to 6
Outputs:
- update: float32 [3, 16, 64, 32], P(None, 'gz', 'gy')
- residual: float32 [3, 16, 64, 32], P(None, 'gz', 'gy')
All inputs are finite; a program needn't handle non-finite values.
Results may differ from a plain program's by a relative error of at most 0.0031.
Values sent between devices are 32-bit elements; how exact they have to be, the bound alone decides.
No kernel may reach another device: no remote copies, remote signals or barrier semaphores. Data moves between devices by JAX's collectives and lax.ppermute only.
A program may use at most 64 MiB of HBM per device.

v0:
```python
import jax
import jax.numpy as jnp
from jax import lax
from jax.sharding import PartitionSpec as P

SPACING = 8
ITERS = 2
damping_weight = 8.0


def from_behind(value, axis, steps):
    count = lax.axis_size(axis)
    initial, last = (max(0, -steps), min(count, count - steps))
    return lax.ppermute(value, axis, [(source, source + steps) for source in range(initial, last)])


def padded_2(cells, sides, width):
    for axis, dim in sides:
        count = lax.axis_size(axis)
        ends = count - 1
        head = lax.slice_in_dim(cells, 0, width, axis=dim)
        tail = lax.slice_in_dim(cells, cells.shape[dim] - width, cells.shape[dim], axis=dim)
        cells = jnp.concatenate(
            [
                lax.ppermute(tail, axis, [(i, (i + 1) % count) for i in range(ends)]),
                cells,
                lax.ppermute(head, axis, [((i + 1) % count, i) for i in range(ends)]),
            ],
            axis=dim,
        )
    return cells


def basis_matrix(count, columns, offset):
    voxel = jnp.arange(count, dtype=jnp.int32)
    cell = voxel // SPACING
    frac = ((voxel % SPACING).astype(jnp.float32) + 0.5) / SPACING
    other = 1.0 - frac
    weights = (
        other**3 / 6.0,
        (3.0 * frac**3 - 6.0 * frac**2 + 4.0) / 6.0,
        (-3.0 * frac**3 + 3.0 * frac**2 + 3.0 * frac + 1.0) / 6.0,
        frac**3 / 6.0,
    )
    index = jnp.arange(columns, dtype=jnp.int32)
    matrix = jnp.zeros((count, columns), jnp.float32)
    for tap in range(4):
        match = index[None, :] == (cell - 1 + tap + offset)[:, None]
        matrix = matrix + jnp.where(match, weights[tap][:, None], jnp.float32(0.0))
    return matrix


def decode(control, along_z, along_y, along_x):
    hp = lax.Precision.HIGHEST
    inner = jnp.einsum("cabe,xe->cabx", control, along_x, precision=hp)
    inner = jnp.einsum("yb,cabx->cayx", along_y, inner, precision=hp)
    return jnp.einsum("za,cayx->czyx", along_z, inner, precision=hp)


def encode(volume, along_z, along_y, along_x):
    hp = lax.Precision.HIGHEST
    inner = jnp.einsum("za,czyx->cayx", along_z, volume, precision=hp)
    inner = jnp.einsum("yb,cayx->cabx", along_y, inner, precision=hp)
    return jnp.einsum("xe,cabx->cabe", along_x, inner, precision=hp)


def derivative(padded, axis):
    length = padded.shape[axis] - 6

    def part(shift_by):
        return lax.slice_in_dim(padded, 3 + shift_by, 3 + shift_by + length, axis=axis)

    return (45.0 * (part(1) - part(-1)) - 9.0 * (part(2) - part(-2)) + (part(3) - part(-3))) / 60.0


def fold_rims(extended):
    depth = extended.shape[1] - 4
    from_above = from_behind(extended[:, 0:2], "gz", -1)
    from_below = from_behind(extended[:, depth + 2 : depth + 4], "gz", 1)
    core = extended[:, 2 : depth + 2]
    core = core.at[:, depth - 2 :].add(from_above).at[:, :2].add(from_below)
    width = core.shape[2] - 4
    from_right = from_behind(core[:, :, 0:2], "gy", -1)
    from_left = from_behind(core[:, :, width + 2 : width + 4], "gy", 1)
    inner = core[:, :, 2 : width + 2]
    return inner.at[:, :, width - 2 :].add(from_right).at[:, :, :2].add(from_left)


def two_products(residual, image):
    return lax.psum((jnp.sum(residual * residual), jnp.sum(residual * image)), ("gz", "gy"))


def shards(fixed, moving):
    slab_z, slab_y, extent = fixed.shape
    pair = jnp.stack([fixed, moving])
    framed = padded_2(pair, (("gz", 1), ("gy", 2)), 3)
    framed = 0.5 * (framed[0] + framed[1])
    framed = jnp.pad(framed, ((0, 0), (0, 0), (3, 3)))
    gradient = jnp.stack(
        [
            derivative(framed[:, 3:-3, 3:-3], 0),
            derivative(framed[3:-3, :, 3:-3], 1),
            derivative(framed[3:-3, 3:-3, :], 2),
        ]
    ).astype(jnp.bfloat16)
    mismatch = moving - fixed
    ctrl_z = slab_z // SPACING
    ctrl_y = slab_y // SPACING
    ctrl_x = extent // SPACING
    along_z = basis_matrix(slab_z, ctrl_z + 4, 2)
    along_y = basis_matrix(slab_y, ctrl_y + 4, 2)
    along_x = basis_matrix(extent, ctrl_x, 0)
    slopes = gradient.astype(jnp.float32)

    def operate(control):
        extended = padded_2(control, (("gz", 1), ("gy", 2)), 2)
        field = decode(extended, along_z, along_y, along_x)
        volume = slopes * jnp.sum(slopes * field, axis=0)[None]
        return fold_rims(encode(volume, along_z, along_y, along_x)) + damping_weight * control

    rhs = -fold_rims(encode(slopes * mismatch[None], along_z, along_y, along_x))
    update = jnp.zeros_like(rhs)
    residual = rhs
    image = operate(residual)
    norm_now, product = two_products(residual, image)
    alpha = norm_now / product
    direction, along = (residual, image)
    for step_index in range(ITERS):
        update = update + alpha * direction
        residual = residual - alpha * along
        if step_index + 1 < ITERS:
            image = operate(residual)
            norm_next, product = two_products(residual, image)
            ratio = norm_next / norm_now
            alpha = norm_next / (product - ratio * norm_next / alpha)
            direction = residual + ratio * direction
            along = image + ratio * along
            norm_now = norm_next
    return (update, residual)


def solution(mesh):
    return jax.shard_map(
        shards,
        mesh=mesh,
        in_specs=(P("gz", "gy", None), P("gz", "gy", None)),
        out_specs=(P(None, "gz", "gy", None), P(None, "gz", "gy", None)),
        check_vma=False,
    )
```

profile of v0, /device:TPU:0, one launch (start us, length us, event | category | flops | bytes accessed | tf_op | source)
XLA Modules:
  0.0 264.6 jit_solution(10514513862206553743)
XLA Ops:
  0.6 4.7 %copy_bitcast_fusion = (f32[1,32,64,256]{3,1,2,0:T(8,128)S(1)}, f32[1,32,64,256]{3,1,2,0:T(8,128)S(1)}) fusion(f32[32,64,256]{2,1,0:T(8,128)} %param.27, f32[32,64,256]{2,1,0:T(8,128)} %param.26), kind=kLoop, calls=%fused_computation.51 | loop fusion | bytes 8388608 | tf_op jit(solution)/shard_map/stack | solution.py:95
  5.5 4.9 %collective-permute-start = (f32[2,3,64,256]{3,1,2,0:T(4,128)S(1)}, f32[2,3,64,256]{3,1,2,0:T(4,128)S(1)}, u32[]{:S(2)}, u32[]{:S(2)}) collective-permute-start(f32[2,3,64,256]{3,1,2,0:T(4,128)S(1)} %get-tuple-element.156), channel_id=1, source_target_pairs={{0,8},{8,16},{16,24},{1,9},{9,17},{17,25},{2,10},{10,18},{18,26},{... | collective-permute-start | bytes 1179656 | tf_op jit(solution)/shard_map/ppermute | solution.py:25
  10.4 1.3 collective-permute-start.1
  11.8 9.7 %collective-permute-done = f32[2,3,64,256]{3,1,2,0:T(4,128)S(1)} collective-permute-done((f32[2,3,64,256]{3,1,2,0:T(4,128)S(1)}, f32[2,3,64,256]{3,1,2,0:T(4,128)S(1)}, u32[]{:S(2)}, u32[]{:S(2)}) %collective-permute-start) | collective-permute-done | bytes 393248 | tf_op jit(solution)/shard_map/ppermute | solution.py:25
  21.5 13.2 %collective-permute-done.1 = f32[2,3,64,256]{3,1,2,0:T(4,128)S(1)} collective-permute-done((f32[2,3,64,256]{3,1,2,0:T(4,128)S(1)}, f32[2,3,64,256]{3,1,2,0:T(4,128)S(1)}, u32[]{:S(2)}, u32[]{:S(2)}) %collective-permute-start.1) | collective-permute-done | bytes 393248 | tf_op jit(solution)/shard_map/ppermute | solution.py:27
  34.8 1.3 collective-permute-start.2
  36.1 1.8 collective-permute-start.3
  38.2 2.6 copy.6
  42.7 8.0 %fusion.51 = (bf16[1,32,64,256]{3,1,2,0:T(8,128)(2,1)}, bf16[1,32,64,256]{3,1,2,0:T(8,128)(2,1)}, bf16[1,32,64,256]{3,1,2,0:T(8,128)(2,1)}) fusion(f32[38,70,256]{2,0,1:T(8,128)S(1)} %fusion.9), kind=kLoop, calls=%fused_computation.69 | loop fusion | flops 14155776 | bytes 31178752 | tf_op jit(solution)/shard_map/stack | solution.py:99
  50.7 6.4 %fusion.41 = f32[3,8,64,256]{3,1,2,0:T(8,128)S(1)} fusion(f32[32,64,256]{2,0,1:T(8,128)} %copy.6, f32[32]{0:T(128)S(1)} %get-tuple-element.198, s32[32]{0:T(128)S(1)} %get-tuple-element.203, f32[32]{0:T(128)S(1)} %get-tuple-element.190, s32[32]{0:T(128)S(1)} %get-tuple-element.205, f32[32]{0:T(128)S(1)} %get-tuple-element.197, ...), kind=kOutput, calls=%fused_computation.63 | convolution fusion | flops 157289216 | bytes 6816768 | tf_op jit(solution)/shard_map/za,czyx->cayx/dot_general | solution.py:62
  57.1 1.3 fusion.42
  58.9 1.4 collective-permute-start.4
  60.4 4.5 %collective-permute-start.5 = (f32[3,2,12,32]{3,2,1,0:T(8,128)S(1)}, f32[3,2,12,32]{3,2,1,0:T(8,128)S(1)}, u32[]{:S(2)}, u32[]{:S(2)}) collective-permute-start(f32[3,2,12,32]{3,2,1,0:T(8,128)S(1)} %get-tuple-element.165), channel_id=1, source_target_pairs={{0,8},{8,16},{16,24},{1,9},{9,17},{17,25},{2,10},{10,18},{18,26},{... | collective-permute-start | bytes 27656 | tf_op jit(solution)/shard_map/ppermute | solution.py:14
  65.1 1.6 collective-permute-done.5
  66.7 1.3 collective-permute-start.6
  68.0 6.2 %collective-permute-start.7 = (f32[3,4,2,32]{3,2,1,0:T(2,128)S(1)}, f32[3,4,2,32]{3,2,1,0:T(2,128)S(1)}, u32[]{:S(2)}, u32[]{:S(2)}) collective-permute-start(f32[3,4,2,32]{3,2,1,0:T(2,128)S(1)} %get-tuple-element.177), channel_id=1, source_target_pairs={{0,1},{1,2},{2,3},{3,4},{4,5},{5,6},{6,7},{8,9},{9,10},{10,11},{11... | collective-permute-start | bytes 9224 | tf_op jit(solution)/shard_map/ppermute | solution.py:14
  74.9 4.3 %collective-permute-start.8 = (f32[3,2,8,32]{3,2,1,0:T(8,128)S(1)}, f32[3,2,8,32]{3,2,1,0:T(8,128)S(1)}, u32[]{:S(2)}, u32[]{:S(2)}) collective-permute-start(f32[3,2,8,32]{3,2,1,0:T(8,128)S(1)} %get-tuple-element.181), channel_id=1, source_target_pairs={{0,8},{8,16},{16,24},{1,9},{9,17},{17,25},{2,10},{10,18},{18,26},{... | collective-permute-start | bytes 18440 | tf_op jit(solution)/shard_map/ppermute | solution.py:25
  79.2 1.3 collective-permute-start.9
  80.7 5.1 %collective-permute-done.9 = f32[3,2,8,32]{3,2,1,0:T(8,128)S(1)} collective-permute-done((f32[3,2,8,32]{3,2,1,0:T(8,128)S(1)}, f32[3,2,8,32]{3,2,1,0:T(8,128)S(1)}, u32[]{:S(2)}, u32[]{:S(2)}) %collective-permute-start.9) | collective-permute-done | bytes 6176 | tf_op jit(solution)/shard_map/ppermute | solution.py:27
  85.9 2.5 collective-permute-start.10
  88.4 1.3 collective-permute-start.11
  89.7 4.7 %collective-permute-done.11 = f32[3,8,2,32]{3,2,1,0:T(2,128)S(1)} collective-permute-done((f32[3,8,2,32]{3,2,1,0:T(2,128)S(1)}, f32[3,8,2,32]{3,2,1,0:T(2,128)S(1)}, u32[]{:S(2)}, u32[]{:S(2)}) %collective-permute-start.11) | collective-permute-done | bytes 6176 | tf_op jit(solution)/shard_map/ppermute | solution.py:27
  94.9 1.4 convolution_bitcast_fusion.1
  96.4 6.1 %fusion.1 = f32[32,64,256]{2,0,1:T(8,128)S(1)} fusion(f32[3,8,64,256]{3,2,1,0:T(8,128)S(1)} %convolution_bitcast_fusion.1, f32[32]{0:T(128)S(1)} %get-tuple-element.198, s32[32]{0:T(128)S(1)} %get-tuple-element.203, f32[32]{0:T(128)S(1)} %get-tuple-element.190, s32[32]{0:T(128)S(1)} %get-tuple-element.205, f32[32]{0:T(128)S(1)} %get-tuple-element.197, ...), kind=kOutput, calls=%fused_computation.12 | convolution fusion | flops 158337792 | bytes 6816768 | tf_op jit(solution)/shard_map/za,cayx->czyx/dot_general | solution.py:57
  102.5 4.1 %fusion.40 = f32[3,8,64,256]{3,1,2,0:T(8,128)S(1)} fusion(f32[32,64,256]{2,0,1:T(8,128)S(1)} %fusion.1, f32[32]{0:T(128)S(1)} %get-tuple-element.198, s32[32]{0:T(128)S(1)} %get-tuple-element.203, f32[32]{0:T(128)S(1)} %get-tuple-element.190, s32[32]{0:T(128)S(1)} %get-tuple-element.205, f32[32]{0:T(128)S(1)} %get-tuple-element.197, ...), kind=kOutput, calls=%fused_computation.62 | convolution fusion | flops 157289216 | bytes 6816768 | tf_op jit(solution)/shard_map/za,czyx->cayx/dot_general | solution.py:62
  106.5 1.3 fusion.45
  108.4 1.3 collective-permute-start.12
  109.7 5.4 %collective-permute-start.13 = (f32[3,2,12,32]{3,2,1,0:T(8,128)S(1)}, f32[3,2,12,32]{3,2,1,0:T(8,128)S(1)}, u32[]{:S(2)}, u32[]{:S(2)}) collective-permute-start(f32[3,2,12,32]{3,2,1,0:T(8,128)S(1)} %get-tuple-element.163), channel_id=1, source_target_pairs={{0,8},{8,16},{16,24},{1,9},{9,17},{17,25},{2,10},{10,18},{18,26},{... | collective-permute-start | bytes 27656 | tf_op jit(solution)/shard_map/ppermute | solution.py:14
  115.3 1.6 collective-permute-done.13
  116.9 1.3 collective-permute-start.14
  118.2 4.2 %collective-permute-start.15 = (f32[3,4,2,32]{3,2,1,0:T(2,128)S(1)}, f32[3,4,2,32]{3,2,1,0:T(2,128)S(1)}, u32[]{:S(2)}, u32[]{:S(2)}) collective-permute-start(f32[3,4,2,32]{3,2,1,0:T(2,128)S(1)} %get-tuple-element.173), channel_id=1, source_target_pairs={{0,1},{1,2},{2,3},{3,4},{4,5},{5,6},{6,7},{8,9},{9,10},{10,11},{11... | collective-permute-start | bytes 9224 | tf_op jit(solution)/shard_map/ppermute | solution.py:14
  123.9 44.3 %all-reduce.2 = (f32[]{:T(128)}, f32[]{:T(128)}) all-reduce(f32[]{:T(128)} %get-tuple-element.149, f32[]{:T(128)} %get-tuple-element.148), channel_id=1, replica_groups=mesh['gz'=4,'gy'=8] {'gz','gy'}, use_global_device_ids=true, to_apply=%region_1.2 | all-reduce | flops 2 | bytes 16 | tf_op jit(solution)/shard_map/psum | solution.py:90
  169.6 4.2 %collective-permute-start.16 = (f32[3,2,8,32]{3,2,1,0:T(8,128)S(1)}, f32[3,2,8,32]{3,2,1,0:T(8,128)S(1)}, u32[]{:S(2)}, u32[]{:S(2)}) collective-permute-start(f32[3,2,8,32]{3,2,1,0:T(8,128)S(1)} %get-tuple-element.179), channel_id=1, source_target_pairs={{0,8},{8,16},{16,24},{1,9},{9,17},{17,25},{2,10},{10,18},{18,26},{... | collective-permute-start | bytes 18440 | tf_op jit(solution)/shard_map/ppermute | solution.py:25
  173.8 1.3 collective-permute-start.17
  175.3 4.2 %collective-permute-done.17 = f32[3,2,8,32]{3,2,1,0:T(8,128)S(1)} collective-permute-done((f32[3,2,8,32]{3,2,1,0:T(8,128)S(1)}, f32[3,2,8,32]{3,2,1,0:T(8,128)S(1)}, u32[]{:S(2)}, u32[]{:S(2)}) %collective-permute-start.17) | collective-permute-done | bytes 6176 | tf_op jit(solution)/shard_map/ppermute | solution.py:27
  179.6 1.5 collective-permute-start.18
  181.1 1.3 collective-permute-start.19
  182.4 3.5 %collective-permute-done.19 = f32[3,8,2,32]{3,2,1,0:T(2,128)S(1)} collective-permute-done((f32[3,8,2,32]{3,2,1,0:T(2,128)S(1)}, f32[3,8,2,32]{3,2,1,0:T(2,128)S(1)}, u32[]{:S(2)}, u32[]{:S(2)}) %collective-permute-start.19) | collective-permute-done | bytes 6176 | tf_op jit(solution)/shard_map/ppermute | solution.py:27
  186.3 1.4 convolution_bitcast_fusion
  187.8 6.1 %fusion.3 = f32[32,64,256]{2,0,1:T(8,128)S(1)} fusion(f32[3,8,64,256]{3,2,1,0:T(8,128)S(1)} %convolution_bitcast_fusion, f32[32]{0:T(128)S(1)} %get-tuple-element.198, s32[32]{0:T(128)S(1)} %get-tuple-element.203, f32[32]{0:T(128)S(1)} %get-tuple-element.190, s32[32]{0:T(128)S(1)} %get-tuple-element.205, f32[32]{0:T(128)S(1)} %get-tuple-element.197, ...), kind=kOutput, calls=%fused_computation.14 | convolution fusion | flops 158337792 | bytes 6816768 | tf_op jit(solution)/shard_map/za,cayx->czyx/dot_general | solution.py:57
  193.9 4.1 %fusion.39 = f32[3,8,64,256]{3,1,2,0:T(8,128)S(1)} fusion(f32[32,64,256]{2,0,1:T(8,128)S(1)} %fusion.3, f32[32]{0:T(128)S(1)} %get-tuple-element.198, s32[32]{0:T(128)S(1)} %get-tuple-element.203, f32[32]{0:T(128)S(1)} %get-tuple-element.190, s32[32]{0:T(128)S(1)} %get-tuple-element.205, f32[32]{0:T(128)S(1)} %get-tuple-element.197, ...), kind=kOutput, calls=%fused_computation.61 | convolution fusion | flops 157289216 | bytes 6816768 | tf_op jit(solution)/shard_map/za,czyx->cayx/dot_general | solution.py:62
  198.0 1.3 fusion.48
  199.8 1.3 collective-permute-start.20
  201.1 5.1 %collective-permute-start.21 = (f32[3,2,12,32]{3,2,1,0:T(8,128)S(1)}, f32[3,2,12,32]{3,2,1,0:T(8,128)S(1)}, u32[]{:S(2)}, u32[]{:S(2)}) collective-permute-start(f32[3,2,12,32]{3,2,1,0:T(8,128)S(1)} %get-tuple-element.161), channel_id=1, source_target_pairs={{0,8},{8,16},{16,24},{1,9},{9,17},{17,25},{2,10},{10,18},{18,26},{... | collective-permute-start | bytes 27656 | tf_op jit(solution)/shard_map/ppermute | solution.py:14
  206.4 1.6 collective-permute-done.21
  208.0 1.3 collective-permute-start.22
  209.3 4.2 %collective-permute-start.23 = (f32[3,4,2,32]{3,2,1,0:T(2,128)S(1)}, f32[3,4,2,32]{3,2,1,0:T(2,128)S(1)}, u32[]{:S(2)}, u32[]{:S(2)}) collective-permute-start(f32[3,4,2,32]{3,2,1,0:T(2,128)S(1)} %get-tuple-element.169), channel_id=1, source_target_pairs={{0,1},{1,2},{2,3},{3,4},{4,5},{5,6},{6,7},{8,9},{9,10},{10,11},{11... | collective-permute-start | bytes 9224 | tf_op jit(solution)/shard_map/ppermute | solution.py:14
  215.1 44.3 %all-reduce.1 = (f32[]{:T(128)}, f32[]{:T(128)}) all-reduce(f32[]{:T(128)} %get-tuple-element.147, f32[]{:T(128)} %get-tuple-element.146), channel_id=1, replica_groups=mesh['gz'=4,'gy'=8] {'gz','gy'}, use_global_device_ids=true, to_apply=%region_6.7 | all-reduce | flops 2 | bytes 16 | tf_op jit(solution)/shard_map/psum | solution.py:90
  (80 shorter events, 10.1 us)
Async XLA Ops:
  5.5 16.0 %collective-permute-start = (f32[2,3,64,256]{3,1,2,0:T(4,128)S(1)}, f32[2,3,64,256]{3,1,2,0:T(4,128)S(1)}, u32[]{:S(2)}, u32[]{:S(2)}) collective-permute-start(f32[2,3,64,256]{3,1,2,0:T(4,128)S(1)} %get-tuple-element.156), channel_id=1, source_target_pairs={{0,8},{8,16},{16,24},{1,9},{9,17},{17,25},{2,10},{10,18},{18,26},{... | collective-permute-start | bytes 1179656 | tf_op jit(solution)/shard_map/ppermute | solution.py:25
  10.4 24.3 %collective-permute-start.1 = (f32[2,3,64,256]{3,1,2,0:T(4,128)S(1)}, f32[2,3,64,256]{3,1,2,0:T(4,128)S(1)}, u32[]{:S(2)}, u32[]{:S(2)}) collective-permute-start(f32[2,3,64,256]{3,1,2,0:T(4,128)S(1)} %get-tuple-element.157), channel_id=1, source_target_pairs={{8,0},{16,8},{24,16},{9,1},{17,9},{25,17},{10,2},{18,10},{26,18},{... | collective-permute-start | bytes 1179656 | tf_op jit(solution)/shard_map/ppermute | solution.py:27
  11.8 26.1 %copy-start.3 = (f32[32,64,256]{2,1,0:T(8,128)S(1)}, f32[32,64,256]{2,1,0:T(8,128)}, u32[]{:S(2)}) copy-start(f32[32,64,256]{2,1,0:T(8,128)} %param.27) | copy-start | bytes 6291460
  11.8 26.0 %copy-start.4 = (f32[32,64,256]{2,1,0:T(8,128)S(1)}, f32[32,64,256]{2,1,0:T(8,128)}, u32[]{:S(2)}) copy-start(f32[32,64,256]{2,1,0:T(8,128)} %param.26) | copy-start | bytes 6291460
  34.8 6.1 %collective-permute-start.2 = (f32[2,38,3,256]{3,1,2,0:T(8,128)S(1)}, f32[2,38,3,256]{3,1,2,0:T(8,128)S(1)}, u32[]{:S(2)}, u32[]{:S(2)}) collective-permute-start(f32[2,38,3,256]{3,1,2,0:T(8,128)S(1)} %get-tuple-element.154), channel_id=1, source_target_pairs={{0,1},{1,2},{2,3},{3,4},{4,5},{5,6},{6,7},{8,9},{9,10},{10,11},{11... | collective-permute-start | bytes 700424 | tf_op jit(solution)/shard_map/ppermute | solution.py:25
  36.1 5.2 %collective-permute-start.3 = (f32[2,38,3,256]{3,1,2,0:T(8,128)S(1)}, f32[2,38,3,256]{3,1,2,0:T(8,128)S(1)}, u32[]{:S(2)}, u32[]{:S(2)}) collective-permute-start(f32[2,38,3,256]{3,1,2,0:T(8,128)S(1)} %get-tuple-element.155), channel_id=1, source_target_pairs={{1,0},{2,1},{3,2},{4,3},{5,4},{6,5},{7,6},{9,8},{10,9},{11,10},{12... | collective-permute-start | bytes 700424 | tf_op jit(solution)/shard_map/ppermute | solution.py:27
  58.4 37.9 %copy-start = (bf16[1,32,64,256]{3,1,2,0:T(8,128)(2,1)S(1)}, bf16[1,32,64,256]{3,1,2,0:T(8,128)(2,1)}, u32[]{:S(2)}) copy-start(bf16[1,32,64,256]{3,1,2,0:T(8,128)(2,1)} %get-tuple-element.158) | copy-start | bytes 3145732
  58.4 37.9 %copy-start.1 = (bf16[1,32,64,256]{3,1,2,0:T(8,128)(2,1)S(1)}, bf16[1,32,64,256]{3,1,2,0:T(8,128)(2,1)}, u32[]{:S(2)}) copy-start(bf16[1,32,64,256]{3,1,2,0:T(8,128)(2,1)} %get-tuple-element.159) | copy-start | bytes 3145732
  58.4 37.9 %copy-start.2 = (bf16[1,32,64,256]{3,1,2,0:T(8,128)(2,1)S(1)}, bf16[1,32,64,256]{3,1,2,0:T(8,128)(2,1)}, u32[]{:S(2)}) copy-start(bf16[1,32,64,256]{3,1,2,0:T(8,128)(2,1)} %get-tuple-element.160) | copy-start | bytes 3145732
  58.9 6.1 %collective-permute-start.4 = (f32[3,2,12,32]{3,2,1,0:T(8,128)S(1)}, f32[3,2,12,32]{3,2,1,0:T(8,128)S(1)}, u32[]{:S(2)}, u32[]{:S(2)}) collective-permute-start(f32[3,2,12,32]{3,2,1,0:T(8,128)S(1)} %get-tuple-element.166), channel_id=1, source_target_pairs={{8,0},{16,8},{24,16},{9,1},{17,9},{25,17},{10,2},{18,10},{26,18},{... | collective-permute-start | bytes 27656 | tf_op jit(solution)/shard_map/ppermute | solution.py:14
  60.4 6.3 %collective-permute-start.5 = (f32[3,2,12,32]{3,2,1,0:T(8,128)S(1)}, f32[3,2,12,32]{3,2,1,0:T(8,128)S(1)}, u32[]{:S(2)}, u32[]{:S(2)}) collective-permute-start(f32[3,2,12,32]{3,2,1,0:T(8,128)S(1)} %get-tuple-element.165), channel_id=1, source_target_pairs={{0,8},{8,16},{16,24},{1,9},{9,17},{17,25},{2,10},{10,18},{18,26},{... | collective-permute-start | bytes 27656 | tf_op jit(solution)/shard_map/ppermute | solution.py:14
  66.7 7.5 %collective-permute-start.6 = (f32[3,4,2,32]{3,2,1,0:T(2,128)S(1)}, f32[3,4,2,32]{3,2,1,0:T(2,128)S(1)}, u32[]{:S(2)}, u32[]{:S(2)}) collective-permute-start(f32[3,4,2,32]{3,2,1,0:T(2,128)S(1)} %get-tuple-element.178), channel_id=1, source_target_pairs={{1,0},{2,1},{3,2},{4,3},{5,4},{6,5},{7,6},{9,8},{10,9},{11,10},{12... | collective-permute-start | bytes 9224 | tf_op jit(solution)/shard_map/ppermute | solution.py:14
  68.0 6.8 %collective-permute-start.7 = (f32[3,4,2,32]{3,2,1,0:T(2,128)S(1)}, f32[3,4,2,32]{3,2,1,0:T(2,128)S(1)}, u32[]{:S(2)}, u32[]{:S(2)}) collective-permute-start(f32[3,4,2,32]{3,2,1,0:T(2,128)S(1)} %get-tuple-element.177), channel_id=1, source_target_pairs={{0,1},{1,2},{2,3},{3,4},{4,5},{5,6},{6,7},{8,9},{9,10},{10,11},{11... | collective-permute-start | bytes 9224 | tf_op jit(solution)/shard_map/ppermute | solution.py:14
  74.9 5.8 %collective-permute-start.8 = (f32[3,2,8,32]{3,2,1,0:T(8,128)S(1)}, f32[3,2,8,32]{3,2,1,0:T(8,128)S(1)}, u32[]{:S(2)}, u32[]{:S(2)}) collective-permute-start(f32[3,2,8,32]{3,2,1,0:T(8,128)S(1)} %get-tuple-element.181), channel_id=1, source_target_pairs={{0,8},{8,16},{16,24},{1,9},{9,17},{17,25},{2,10},{10,18},{18,26},{... | collective-permute-start | bytes 18440 | tf_op jit(solution)/shard_map/ppermute | solution.py:25
  79.2 6.7 %collective-permute-start.9 = (f32[3,2,8,32]{3,2,1,0:T(8,128)S(1)}, f32[3,2,8,32]{3,2,1,0:T(8,128)S(1)}, u32[]{:S(2)}, u32[]{:S(2)}) collective-permute-start(f32[3,2,8,32]{3,2,1,0:T(8,128)S(1)} %get-tuple-element.182), channel_id=1, source_target_pairs={{8,0},{16,8},{24,16},{9,1},{17,9},{25,17},{10,2},{18,10},{26,18},{... | collective-permute-start | bytes 18440 | tf_op jit(solution)/shard_map/ppermute | solution.py:27
  85.9 3.8 %collective-permute-start.10 = (f32[3,8,2,32]{3,2,1,0:T(2,128)S(1)}, f32[3,8,2,32]{3,2,1,0:T(2,128)S(1)}, u32[]{:S(2)}, u32[]{:S(2)}) collective-permute-start(f32[3,8,2,32]{3,2,1,0:T(2,128)S(1)} %get-tuple-element.175), channel_id=1, source_target_pairs={{0,1},{1,2},{2,3},{3,4},{4,5},{5,6},{6,7},{8,9},{9,10},{10,11},{11... | collective-permute-start | bytes 18440 | tf_op jit(solution)/shard_map/ppermute | solution.py:25
  88.4 6.0 %collective-permute-start.11 = (f32[3,8,2,32]{3,2,1,0:T(2,128)S(1)}, f32[3,8,2,32]{3,2,1,0:T(2,128)S(1)}, u32[]{:S(2)}, u32[]{:S(2)}) collective-permute-start(f32[3,8,2,32]{3,2,1,0:T(2,128)S(1)} %get-tuple-element.176), channel_id=1, source_target_pairs={{1,0},{2,1},{3,2},{4,3},{5,4},{6,5},{7,6},{9,8},{10,9},{11,10},{12... | collective-permute-start | bytes 18440 | tf_op jit(solution)/shard_map/ppermute | solution.py:27
  108.4 6.9 %collective-permute-start.12 = (f32[3,2,12,32]{3,2,1,0:T(8,128)S(1)}, f32[3,2,12,32]{3,2,1,0:T(8,128)S(1)}, u32[]{:S(2)}, u32[]{:S(2)}) collective-permute-start(f32[3,2,12,32]{3,2,1,0:T(8,128)S(1)} %get-tuple-element.164), channel_id=1, source_target_pairs={{8,0},{16,8},{24,16},{9,1},{17,9},{25,17},{10,2},{18,10},{26,18},{... | collective-permute-start | bytes 27656 | tf_op jit(solution)/shard_map/ppermute | solution.py:14
  109.7 7.2 %collective-permute-start.13 = (f32[3,2,12,32]{3,2,1,0:T(8,128)S(1)}, f32[3,2,12,32]{3,2,1,0:T(8,128)S(1)}, u32[]{:S(2)}, u32[]{:S(2)}) collective-permute-start(f32[3,2,12,32]{3,2,1,0:T(8,128)S(1)} %get-tuple-element.163), channel_id=1, source_target_pairs={{0,8},{8,16},{16,24},{1,9},{9,17},{17,25},{2,10},{10,18},{18,26},{... | collective-permute-start | bytes 27656 | tf_op jit(solution)/shard_map/ppermute | solution.py:14
  116.9 5.6 %collective-permute-start.14 = (f32[3,4,2,32]{3,2,1,0:T(2,128)S(1)}, f32[3,4,2,32]{3,2,1,0:T(2,128)S(1)}, u32[]{:S(2)}, u32[]{:S(2)}) collective-permute-start(f32[3,4,2,32]{3,2,1,0:T(2,128)S(1)} %get-tuple-element.174), channel_id=1, source_target_pairs={{1,0},{2,1},{3,2},{4,3},{5,4},{6,5},{7,6},{9,8},{10,9},{11,10},{12... | collective-permute-start | bytes 9224 | tf_op jit(solution)/shard_map/ppermute | solution.py:14
  118.2 5.1 %collective-permute-start.15 = (f32[3,4,2,32]{3,2,1,0:T(2,128)S(1)}, f32[3,4,2,32]{3,2,1,0:T(2,128)S(1)}, u32[]{:S(2)}, u32[]{:S(2)}) collective-permute-start(f32[3,4,2,32]{3,2,1,0:T(2,128)S(1)} %get-tuple-element.173), channel_id=1, source_target_pairs={{0,1},{1,2},{2,3},{3,4},{4,5},{5,6},{6,7},{8,9},{9,10},{10,11},{11... | collective-permute-start | bytes 9224 | tf_op jit(solution)/shard_map/ppermute | solution.py:14
  169.6 5.7 %collective-permute-start.16 = (f32[3,2,8,32]{3,2,1,0:T(8,128)S(1)}, f32[3,2,8,32]{3,2,1,0:T(8,128)S(1)}, u32[]{:S(2)}, u32[]{:S(2)}) collective-permute-start(f32[3,2,8,32]{3,2,1,0:T(8,128)S(1)} %get-tuple-element.179), channel_id=1, source_target_pairs={{0,8},{8,16},{16,24},{1,9},{9,17},{17,25},{2,10},{10,18},{18,26},{... | collective-permute-start | bytes 18440 | tf_op jit(solution)/shard_map/ppermute | solution.py:25
  173.8 5.7 %collective-permute-start.17 = (f32[3,2,8,32]{3,2,1,0:T(8,128)S(1)}, f32[3,2,8,32]{3,2,1,0:T(8,128)S(1)}, u32[]{:S(2)}, u32[]{:S(2)}) collective-permute-start(f32[3,2,8,32]{3,2,1,0:T(8,128)S(1)} %get-tuple-element.180), channel_id=1, source_target_pairs={{8,0},{16,8},{24,16},{9,1},{17,9},{25,17},{10,2},{18,10},{26,18},{... | collective-permute-start | bytes 18440 | tf_op jit(solution)/shard_map/ppermute | solution.py:27
  179.6 2.8 %collective-permute-start.18 = (f32[3,8,2,32]{3,2,1,0:T(2,128)S(1)}, f32[3,8,2,32]{3,2,1,0:T(2,128)S(1)}, u32[]{:S(2)}, u32[]{:S(2)}) collective-permute-start(f32[3,8,2,32]{3,2,1,0:T(2,128)S(1)} %get-tuple-element.171), channel_id=1, source_target_pairs={{0,1},{1,2},{2,3},{3,4},{4,5},{5,6},{6,7},{8,9},{9,10},{10,11},{11... | collective-permute-start | bytes 18440 | tf_op jit(solution)/shard_map/ppermute | solution.py:25
  181.1 4.8 %collective-permute-start.19 = (f32[3,8,2,32]{3,2,1,0:T(2,128)S(1)}, f32[3,8,2,32]{3,2,1,0:T(2,128)S(1)}, u32[]{:S(2)}, u32[]{:S(2)}) collective-permute-start(f32[3,8,2,32]{3,2,1,0:T(2,128)S(1)} %get-tuple-element.172), channel_id=1, source_target_pairs={{1,0},{2,1},{3,2},{4,3},{5,4},{6,5},{7,6},{9,8},{10,9},{11,10},{12... | collective-permute-start | bytes 18440 | tf_op jit(solution)/shard_map/ppermute | solution.py:27
  199.8 6.5 %collective-permute-start.20 = (f32[3,2,12,32]{3,2,1,0:T(8,128)S(1)}, f32[3,2,12,32]{3,2,1,0:T(8,128)S(1)}, u32[]{:S(2)}, u32[]{:S(2)}) collective-permute-start(f32[3,2,12,32]{3,2,1,0:T(8,128)S(1)} %get-tuple-element.162), channel_id=1, source_target_pairs={{8,0},{16,8},{24,16},{9,1},{17,9},{25,17},{10,2},{18,10},{26,18},{... | collective-permute-start | bytes 27656 | tf_op jit(solution)/shard_map/ppermute | solution.py:14
  201.1 6.8 %collective-permute-start.21 = (f32[3,2,12,32]{3,2,1,0:T(8,128)S(1)}, f32[3,2,12,32]{3,2,1,0:T(8,128)S(1)}, u32[]{:S(2)}, u32[]{:S(2)}) collective-permute-start(f32[3,2,12,32]{3,2,1,0:T(8,128)S(1)} %get-tuple-element.161), channel_id=1, source_target_pairs={{0,8},{8,16},{16,24},{1,9},{9,17},{17,25},{2,10},{10,18},{18,26},{... | collective-permute-start | bytes 27656 | tf_op jit(solution)/shard_map/ppermute | solution.py:14
  208.0 5.6 %collective-permute-start.22 = (f32[3,4,2,32]{3,2,1,0:T(2,128)S(1)}, f32[3,4,2,32]{3,2,1,0:T(2,128)S(1)}, u32[]{:S(2)}, u32[]{:S(2)}) collective-permute-start(f32[3,4,2,32]{3,2,1,0:T(2,128)S(1)} %get-tuple-element.170), channel_id=1, source_target_pairs={{1,0},{2,1},{3,2},{4,3},{5,4},{6,5},{7,6},{9,8},{10,9},{11,10},{12... | collective-permute-start | bytes 9224 | tf_op jit(solution)/shard_map/ppermute | solution.py:14
  209.3 5.1 %collective-permute-start.23 = (f32[3,4,2,32]{3,2,1,0:T(2,128)S(1)}, f32[3,4,2,32]{3,2,1,0:T(2,128)S(1)}, u32[]{:S(2)}, u32[]{:S(2)}) collective-permute-start(f32[3,4,2,32]{3,2,1,0:T(2,128)S(1)} %get-tuple-element.169), channel_id=1, source_target_pairs={{0,1},{1,2},{2,3},{3,4},{4,5},{5,6},{6,7},{8,9},{9,10},{10,11},{11... | collective-permute-start | bytes 9224 | tf_op jit(solution)/shard_map/ppermute | solution.py:14
where the time goes:
time: 269 us; the launch traced here: 265 us
  blocking collectives  88.6 us (33%)
  starting transfers between devices  64.5 us (24%)
  waiting for transfers between devices  48.6 us (18%)
  matrix products  35.9 us (13%)
  other arithmetic  12.3 us (5%)
  local copies, waits for them, and re-layouts  7.36 us (3%)
  between operations  7.22 us (3%)
    psum x2, blocking collectives, two_products(): lax.psum((jnp.sum(residual * residual), jnp.sum(residual * image)), ('gz'...  88.6 us
    ppermute x12, starting transfers between devices, from_behind(): lax.ppermute(value, axis, [(source, source + steps) for source in range(i...  37.6 us
    ppermute x6, waiting for transfers between devices, padded_2(): lax.ppermute(head, axis, [((i + 1) % count, i) for i in range(ends)])  31.2 us
    ppermute x6, starting transfers between devices, padded_2(): lax.ppermute(tail, axis, [(i, (i + 1) % count) for i in range(ends)])  18.7 us
    dot_general x3, matrix products, encode(): inner = jnp.einsum('za,czyx->cayx', along_z, volume, precision=hp)  14.5 us
    dot_general x2, matrix products, decode(): return jnp.einsum('za,cayx->czyx', along_z, inner, precision=hp)  12.2 us
    ppermute x6, waiting for transfers between devices, padded_2(): lax.ppermute(tail, axis, [(i, (i + 1) % count) for i in range(ends)])  10.1 us
    ppermute x6, starting transfers between devices, padded_2(): lax.ppermute(head, axis, [((i + 1) % count, i) for i in range(ends)])  8.22 us
  transfers between devices with their start and end apart: 24, of which 18 were waited for; matrix products, arithmetic and copies ran while one was open for 1% of the time, Pallas kernels for 0%

commit v1 on v0

--- a/solution.py
+++ b/solution.py
@@ -87,7 +87,7 @@
 
 
 def two_products(residual, image):
-    return lax.psum((jnp.sum(residual * residual), jnp.sum(residual * image)), ("gz", "gy"))
+    return lax.psum(lax.psum((jnp.sum(residual * residual), jnp.sum(residual * image)), "gy"), "gz")
 
 
 def shards(fixed, moving):

time: 269 us -> 232 us (0.86)
  blocking collectives: 88.6 us -> 55.9 us
    psum x2 -> x4, blocking collectives: 88.6 us -> 55.9 us  [the longest x2 33.7 us: two_products(): lax.psum((jnp.sum(residual * residual), jnp.sum(residual * image)), 'gy')]
where the time goes in v1:
time: 232 us; the launch traced here: 228 us
  starting transfers between devices  62.4 us (27%)
  blocking collectives  55.9 us (24%)
  waiting for transfers between devices  46.7 us (20%)
  matrix products  35.9 us (15%)
  other arithmetic  12.3 us (5%)
  local copies, waits for them, and re-layouts  7.38 us (3%)
  between operations  7.28 us (3%)
    ppermute x12, starting transfers between devices, from_behind(): lax.ppermute(value, axis, [(source, source + steps) for source in range(i...  35.9 us
    psum x2, blocking collectives, two_products(): lax.psum((jnp.sum(residual * residual), jnp.sum(residual * image)), 'gy')  33.7 us
    ppermute x6, waiting for transfers between devices, padded_2(): lax.ppermute(head, axis, [((i + 1) % count, i) for i in range(ends)])  29.3 us
    psum x2, blocking collectives, two_products(): lax.psum(lax.psum((jnp.sum(residual * residual), jnp.sum(residual * image...  22.1 us
    ppermute x6, starting transfers between devices, padded_2(): lax.ppermute(tail, axis, [(i, (i + 1) % count) for i in range(ends)])  18.1 us
    dot_general x3, matrix products, encode(): inner = jnp.einsum('za,czyx->cayx', along_z, volume, precision=hp)  14.5 us
    dot_general x2, matrix products, decode(): return jnp.einsum('za,cayx->czyx', along_z, inner, precision=hp)  12.2 us
    ppermute x6, waiting for transfers between devices, padded_2(): lax.ppermute(tail, axis, [(i, (i + 1) % count) for i in range(ends)])  10.1 us
  transfers between devices with their start and end apart: 24, of which 18 were waited for; matrix products, arithmetic and copies ran while one was open for 1% of the time, Pallas kernels for 0%

profile of v1, /device:TPU:0, one launch (start us, length us, event | category | flops | bytes accessed | tf_op | source)
XLA Modules:
  0.0 227.9 jit_solution(4259805977871045244)
XLA Ops:
  0.6 4.7 %copy_bitcast_fusion = (f32[1,32,64,256]{3,1,2,0:T(8,128)S(1)}, f32[1,32,64,256]{3,1,2,0:T(8,128)S(1)}) fusion(f32[32,64,256]{2,1,0:T(8,128)} %param.27, f32[32,64,256]{2,1,0:T(8,128)} %param.26), kind=kLoop, calls=%fused_computation.51 | loop fusion | bytes 8388608 | tf_op jit(solution)/shard_map/stack | solution.py:95
  5.5 4.9 %collective-permute-start = (f32[2,3,64,256]{3,1,2,0:T(4,128)S(1)}, f32[2,3,64,256]{3,1,2,0:T(4,128)S(1)}, u32[]{:S(2)}, u32[]{:S(2)}) collective-permute-start(f32[2,3,64,256]{3,1,2,0:T(4,128)S(1)} %get-tuple-element.160), channel_id=1, source_target_pairs={{0,8},{8,16},{16,24},{1,9},{9,17},{17,25},{2,10},{10,18},{18,26},{... | collective-permute-start | bytes 1179656 | tf_op jit(solution)/shard_map/ppermute | solution.py:25
  10.4 1.3 collective-permute-start.1
  11.8 9.7 %collective-permute-done = f32[2,3,64,256]{3,1,2,0:T(4,128)S(1)} collective-permute-done((f32[2,3,64,256]{3,1,2,0:T(4,128)S(1)}, f32[2,3,64,256]{3,1,2,0:T(4,128)S(1)}, u32[]{:S(2)}, u32[]{:S(2)}) %collective-permute-start) | collective-permute-done | bytes 393248 | tf_op jit(solution)/shard_map/ppermute | solution.py:25
  21.5 13.2 %collective-permute-done.1 = f32[2,3,64,256]{3,1,2,0:T(4,128)S(1)} collective-permute-done((f32[2,3,64,256]{3,1,2,0:T(4,128)S(1)}, f32[2,3,64,256]{3,1,2,0:T(4,128)S(1)}, u32[]{:S(2)}, u32[]{:S(2)}) %collective-permute-start.1) | collective-permute-done | bytes 393248 | tf_op jit(solution)/shard_map/ppermute | solution.py:27
  34.8 1.3 collective-permute-start.2
  36.1 1.8 collective-permute-start.3
  38.2 2.6 %copy.6 = f32[32,64,256]{2,0,1:T(8,128)} copy(f32[32,64,256]{2,1,0:T(8,128)S(1)} %sub.214) | data formatting | bytes 4194304 | tf_op jit(solution)/shard_map/sub | solution.py:106
  42.7 8.0 %fusion.51 = (bf16[1,32,64,256]{3,1,2,0:T(8,128)(2,1)}, bf16[1,32,64,256]{3,1,2,0:T(8,128)(2,1)}, bf16[1,32,64,256]{3,1,2,0:T(8,128)(2,1)}) fusion(f32[38,70,256]{2,0,1:T(8,128)S(1)} %fusion.9), kind=kLoop, calls=%fused_computation.69 | loop fusion | flops 14155776 | bytes 31178752 | tf_op jit(solution)/shard_map/stack | solution.py:99
  50.7 6.4 %fusion.41 = f32[3,8,64,256]{3,1,2,0:T(8,128)S(1)} fusion(f32[32,64,256]{2,0,1:T(8,128)} %copy.6, f32[32]{0:T(128)S(1)} %get-tuple-element.202, s32[32]{0:T(128)S(1)} %get-tuple-element.207, f32[32]{0:T(128)S(1)} %get-tuple-element.194, s32[32]{0:T(128)S(1)} %get-tuple-element.209, f32[32]{0:T(128)S(1)} %get-tuple-element.201, ...), kind=kOutput, calls=%fused_computation.63 | convolution fusion | flops 157289216 | bytes 6816768 | tf_op jit(solution)/shard_map/za,czyx->cayx/dot_general | solution.py:62
  57.1 1.3 fusion.42
  59.0 1.4 collective-permute-start.4
  60.4 4.5 %collective-permute-start.5 = (f32[3,2,12,32]{3,2,1,0:T(8,128)S(1)}, f32[3,2,12,32]{3,2,1,0:T(8,128)S(1)}, u32[]{:S(2)}, u32[]{:S(2)}) collective-permute-start(f32[3,2,12,32]{3,2,1,0:T(8,128)S(1)} %get-tuple-element.169), channel_id=1, source_target_pairs={{0,8},{8,16},{16,24},{1,9},{9,17},{17,25},{2,10},{10,18},{18,26},{... | collective-permute-start | bytes 27656 | tf_op jit(solution)/shard_map/ppermute | solution.py:14
  65.1 1.6 collective-permute-done.5
  66.7 1.3 collective-permute-start.6
  68.1 6.2 %collective-permute-start.7 = (f32[3,4,2,32]{3,2,1,0:T(2,128)S(1)}, f32[3,4,2,32]{3,2,1,0:T(2,128)S(1)}, u32[]{:S(2)}, u32[]{:S(2)}) collective-permute-start(f32[3,4,2,32]{3,2,1,0:T(2,128)S(1)} %get-tuple-element.181), channel_id=1, source_target_pairs={{0,1},{1,2},{2,3},{3,4},{4,5},{5,6},{6,7},{8,9},{9,10},{10,11},{11... | collective-permute-start | bytes 9224 | tf_op jit(solution)/shard_map/ppermute | solution.py:14
  74.9 4.3 %collective-permute-start.8 = (f32[3,2,8,32]{3,2,1,0:T(8,128)S(1)}, f32[3,2,8,32]{3,2,1,0:T(8,128)S(1)}, u32[]{:S(2)}, u32[]{:S(2)}) collective-permute-start(f32[3,2,8,32]{3,2,1,0:T(8,128)S(1)} %get-tuple-element.185), channel_id=1, source_target_pairs={{0,8},{8,16},{16,24},{1,9},{9,17},{17,25},{2,10},{10,18},{18,26},{... | collective-permute-start | bytes 18440 | tf_op jit(solution)/shard_map/ppermute | solution.py:25
  79.2 1.3 collective-permute-start.9
  80.7 5.1 %collective-permute-done.9 = f32[3,2,8,32]{3,2,1,0:T(8,128)S(1)} collective-permute-done((f32[3,2,8,32]{3,2,1,0:T(8,128)S(1)}, f32[3,2,8,32]{3,2,1,0:T(8,128)S(1)}, u32[]{:S(2)}, u32[]{:S(2)}) %collective-permute-start.9) | collective-permute-done | bytes 6176 | tf_op jit(solution)/shard_map/ppermute | solution.py:27
  85.9 2.5 %collective-permute-start.10 = (f32[3,8,2,32]{3,2,1,0:T(2,128)S(1)}, f32[3,8,2,32]{3,2,1,0:T(2,128)S(1)}, u32[]{:S(2)}, u32[]{:S(2)}) collective-permute-start(f32[3,8,2,32]{3,2,1,0:T(2,128)S(1)} %get-tuple-element.179), channel_id=1, source_target_pairs={{0,1},{1,2},{2,3},{3,4},{4,5},{5,6},{6,7},{8,9},{9,10},{10,11},{11... | collective-permute-start | bytes 18440 | tf_op jit(solution)/shard_map/ppermute | solution.py:25
  88.4 1.3 collective-permute-start.11
  89.7 4.7 %collective-permute-done.11 = f32[3,8,2,32]{3,2,1,0:T(2,128)S(1)} collective-permute-done((f32[3,8,2,32]{3,2,1,0:T(2,128)S(1)}, f32[3,8,2,32]{3,2,1,0:T(2,128)S(1)}, u32[]{:S(2)}, u32[]{:S(2)}) %collective-permute-start.11) | collective-permute-done | bytes 6176 | tf_op jit(solution)/shard_map/ppermute | solution.py:27
  94.9 1.4 convolution_bitcast_fusion.1
  96.4 6.1 %fusion.1 = f32[32,64,256]{2,0,1:T(8,128)S(1)} fusion(f32[3,8,64,256]{3,2,1,0:T(8,128)S(1)} %convolution_bitcast_fusion.1, f32[32]{0:T(128)S(1)} %get-tuple-element.202, s32[32]{0:T(128)S(1)} %get-tuple-element.207, f32[32]{0:T(128)S(1)} %get-tuple-element.194, s32[32]{0:T(128)S(1)} %get-tuple-element.209, f32[32]{0:T(128)S(1)} %get-tuple-element.201, ...), kind=kOutput, calls=%fused_computation.12 | convolution fusion | flops 158337792 | bytes 6816768 | tf_op jit(solution)/shard_map/za,cayx->czyx/dot_general | solution.py:57
  102.5 4.1 %fusion.40 = f32[3,8,64,256]{3,1,2,0:T(8,128)S(1)} fusion(f32[32,64,256]{2,0,1:T(8,128)S(1)} %fusion.1, f32[32]{0:T(128)S(1)} %get-tuple-element.202, s32[32]{0:T(128)S(1)} %get-tuple-element.207, f32[32]{0:T(128)S(1)} %get-tuple-element.194, s32[32]{0:T(128)S(1)} %get-tuple-element.209, f32[32]{0:T(128)S(1)} %get-tuple-element.201, ...), kind=kOutput, calls=%fused_computation.62 | convolution fusion | flops 157289216 | bytes 6816768 | tf_op jit(solution)/shard_map/za,czyx->cayx/dot_general | solution.py:62
  106.6 1.3 fusion.45
  108.4 1.3 collective-permute-start.12
  109.7 5.4 %collective-permute-start.13 = (f32[3,2,12,32]{3,2,1,0:T(8,128)S(1)}, f32[3,2,12,32]{3,2,1,0:T(8,128)S(1)}, u32[]{:S(2)}, u32[]{:S(2)}) collective-permute-start(f32[3,2,12,32]{3,2,1,0:T(8,128)S(1)} %get-tuple-element.167), channel_id=1, source_target_pairs={{0,8},{8,16},{16,24},{1,9},{9,17},{17,25},{2,10},{10,18},{18,26},{... | collective-permute-start | bytes 27656 | tf_op jit(solution)/shard_map/ppermute | solution.py:14
  115.3 1.6 collective-permute-done.13
  116.9 1.3 collective-permute-start.14
  118.3 4.2 %collective-permute-start.15 = (f32[3,4,2,32]{3,2,1,0:T(2,128)S(1)}, f32[3,4,2,32]{3,2,1,0:T(2,128)S(1)}, u32[]{:S(2)}, u32[]{:S(2)}) collective-permute-start(f32[3,4,2,32]{3,2,1,0:T(2,128)S(1)} %get-tuple-element.177), channel_id=1, source_target_pairs={{0,1},{1,2},{2,3},{3,4},{4,5},{5,6},{6,7},{8,9},{9,10},{10,11},{11... | collective-permute-start | bytes 9224 | tf_op jit(solution)/shard_map/ppermute | solution.py:14
  123.9 17.8 %all-reduce.2 = (f32[]{:T(128)}, f32[]{:T(128)}) all-reduce(f32[]{:T(128)} %get-tuple-element.149, f32[]{:T(128)} %get-tuple-element.148), channel_id=1, replica_groups=mesh['gz'=4,'gy'=8] {'gy'}, use_global_device_ids=true, to_apply=%region_1.2 | all-reduce | flops 2 | bytes 16 | tf_op jit(solution)/shard_map/psum | solution.py:90
  141.8 11.0 %all-reduce.4 = (f32[]{:T(128)}, f32[]{:T(128)}) all-reduce(f32[]{:T(128)} %get-tuple-element.152, f32[]{:T(128)} %get-tuple-element.153), channel_id=1, replica_groups=mesh['gz'=4,'gy'=8] {'gz'}, use_global_device_ids=true, to_apply=%region_2.3 | all-reduce | flops 2 | bytes 16 | tf_op jit(solution)/shard_map/psum | solution.py:90
  154.1 3.8 %collective-permute-start.16 = (f32[3,2,8,32]{3,2,1,0:T(8,128)S(1)}, f32[3,2,8,32]{3,2,1,0:T(8,128)S(1)}, u32[]{:S(2)}, u32[]{:S(2)}) collective-permute-start(f32[3,2,8,32]{3,2,1,0:T(8,128)S(1)} %get-tuple-element.183), channel_id=1, source_target_pairs={{0,8},{8,16},{16,24},{1,9},{9,17},{17,25},{2,10},{10,18},{18,26},{... | collective-permute-start | bytes 18440 | tf_op jit(solution)/shard_map/ppermute | solution.py:25
  158.0 1.3 collective-permute-start.17
  159.5 4.2 %collective-permute-done.17 = f32[3,2,8,32]{3,2,1,0:T(8,128)S(1)} collective-permute-done((f32[3,2,8,32]{3,2,1,0:T(8,128)S(1)}, f32[3,2,8,32]{3,2,1,0:T(8,128)S(1)}, u32[]{:S(2)}, u32[]{:S(2)}) %collective-permute-start.17) | collective-permute-done | bytes 6176 | tf_op jit(solution)/shard_map/ppermute | solution.py:27
  165.0 1.5 collective-permute-start.19
  166.5 1.6 collective-permute-done.19
  168.6 1.4 convolution_bitcast_fusion
  170.0 6.1 %fusion.3 = f32[32,64,256]{2,0,1:T(8,128)S(1)} fusion(f32[3,8,64,256]{3,2,1,0:T(8,128)S(1)} %convolution_bitcast_fusion, f32[32]{0:T(128)S(1)} %get-tuple-element.202, s32[32]{0:T(128)S(1)} %get-tuple-element.207, f32[32]{0:T(128)S(1)} %get-tuple-element.194, s32[32]{0:T(128)S(1)} %get-tuple-element.209, f32[32]{0:T(128)S(1)} %get-tuple-element.201, ...), kind=kOutput, calls=%fused_computation.14 | convolution fusion | flops 158337792 | bytes 6816768 | tf_op jit(solution)/shard_map/za,cayx->czyx/dot_general | solution.py:57
  176.1 4.1 %fusion.39 = f32[3,8,64,256]{3,1,2,0:T(8,128)S(1)} fusion(f32[32,64,256]{2,0,1:T(8,128)S(1)} %fusion.3, f32[32]{0:T(128)S(1)} %get-tuple-element.202, s32[32]{0:T(128)S(1)} %get-tuple-element.207, f32[32]{0:T(128)S(1)} %get-tuple-element.194, s32[32]{0:T(128)S(1)} %get-tuple-element.209, f32[32]{0:T(128)S(1)} %get-tuple-element.201, ...), kind=kOutput, calls=%fused_computation.61 | convolution fusion | flops 157289216 | bytes 6816768 | tf_op jit(solution)/shard_map/za,czyx->cayx/dot_general | solution.py:62
  180.2 1.3 fusion.48
  182.1 1.3 collective-permute-start.20
  183.4 4.5 %collective-permute-start.21 = (f32[3,2,12,32]{3,2,1,0:T(8,128)S(1)}, f32[3,2,12,32]{3,2,1,0:T(8,128)S(1)}, u32[]{:S(2)}, u32[]{:S(2)}) collective-permute-start(f32[3,2,12,32]{3,2,1,0:T(8,128)S(1)} %get-tuple-element.165), channel_id=1, source_target_pairs={{0,8},{8,16},{16,24},{1,9},{9,17},{17,25},{2,10},{10,18},{18,26},{... | collective-permute-start | bytes 27656 | tf_op jit(solution)/shard_map/ppermute | solution.py:14
  189.7 1.3 collective-permute-start.22
  191.0 3.0 %collective-permute-start.23 = (f32[3,4,2,32]{3,2,1,0:T(2,128)S(1)}, f32[3,4,2,32]{3,2,1,0:T(2,128)S(1)}, u32[]{:S(2)}, u32[]{:S(2)}) collective-permute-start(f32[3,4,2,32]{3,2,1,0:T(2,128)S(1)} %get-tuple-element.173), channel_id=1, source_target_pairs={{0,1},{1,2},{2,3},{3,4},{4,5},{5,6},{6,7},{8,9},{9,10},{10,11},{11... | collective-permute-start | bytes 9224 | tf_op jit(solution)/shard_map/ppermute | solution.py:14
  195.5 15.9 %all-reduce.1 = (f32[]{:T(128)}, f32[]{:T(128)}) all-reduce(f32[]{:T(128)} %get-tuple-element.147, f32[]{:T(128)} %get-tuple-element.146), channel_id=1, replica_groups=mesh['gz'=4,'gy'=8] {'gy'}, use_global_device_ids=true, to_apply=%region_8.9 | all-reduce | flops 2 | bytes 16 | tf_op jit(solution)/shard_map/psum | solution.py:90
  211.5 11.1 %all-reduce.3 = (f32[]{:T(128)}, f32[]{:T(128)}) all-reduce(f32[]{:T(128)} %get-tuple-element.150, f32[]{:T(128)} %get-tuple-element.151), channel_id=1, replica_groups=mesh['gz'=4,'gy'=8] {'gz'}, use_global_device_ids=true, to_apply=%region_9.10 | all-reduce | flops 2 | bytes 16 | tf_op jit(solution)/shard_map/psum | solution.py:90
  (82 shorter events, 13.0 us)
Async XLA Ops:
  5.5 16.0 %collective-permute-start = (f32[2,3,64,256]{3,1,2,0:T(4,128)S(1)}, f32[2,3,64,256]{3,1,2,0:T(4,128)S(1)}, u32[]{:S(2)}, u32[]{:S(2)}) collective-permute-start(f32[2,3,64,256]{3,1,2,0:T(4,128)S(1)} %get-tuple-element.160), channel_id=1, source_target_pairs={{0,8},{8,16},{16,24},{1,9},{9,17},{17,25},{2,10},{10,18},{18,26},{... | collective-permute-start | bytes 1179656 | tf_op jit(solution)/shard_map/ppermute | solution.py:25
  10.4 24.3 %collective-permute-start.1 = (f32[2,3,64,256]{3,1,2,0:T(4,128)S(1)}, f32[2,3,64,256]{3,1,2,0:T(4,128)S(1)}, u32[]{:S(2)}, u32[]{:S(2)}) collective-permute-start(f32[2,3,64,256]{3,1,2,0:T(4,128)S(1)} %get-tuple-element.161), channel_id=1, source_target_pairs={{8,0},{16,8},{24,16},{9,1},{17,9},{25,17},{10,2},{18,10},{26,18},{... | collective-permute-start | bytes 1179656 | tf_op jit(solution)/shard_map/ppermute | solution.py:27
  11.8 26.1 %copy-start.3 = (f32[32,64,256]{2,1,0:T(8,128)S(1)}, f32[32,64,256]{2,1,0:T(8,128)}, u32[]{:S(2)}) copy-start(f32[32,64,256]{2,1,0:T(8,128)} %param.27) | copy-start | bytes 6291460
  11.8 26.0 %copy-start.4 = (f32[32,64,256]{2,1,0:T(8,128)S(1)}, f32[32,64,256]{2,1,0:T(8,128)}, u32[]{:S(2)}) copy-start(f32[32,64,256]{2,1,0:T(8,128)} %param.26) | copy-start | bytes 6291460
  34.8 6.1 %collective-permute-start.2 = (f32[2,38,3,256]{3,1,2,0:T(8,128)S(1)}, f32[2,38,3,256]{3,1,2,0:T(8,128)S(1)}, u32[]{:S(2)}, u32[]{:S(2)}) collective-permute-start(f32[2,38,3,256]{3,1,2,0:T(8,128)S(1)} %get-tuple-element.158), channel_id=1, source_target_pairs={{0,1},{1,2},{2,3},{3,4},{4,5},{5,6},{6,7},{8,9},{9,10},{10,11},{11... | collective-permute-start | bytes 700424 | tf_op jit(solution)/shard_map/ppermute | solution.py:25
  36.1 5.2 %collective-permute-start.3 = (f32[2,38,3,256]{3,1,2,0:T(8,128)S(1)}, f32[2,38,3,256]{3,1,2,0:T(8,128)S(1)}, u32[]{:S(2)}, u32[]{:S(2)}) collective-permute-start(f32[2,38,3,256]{3,1,2,0:T(8,128)S(1)} %get-tuple-element.159), channel_id=1, source_target_pairs={{1,0},{2,1},{3,2},{4,3},{5,4},{6,5},{7,6},{9,8},{10,9},{11,10},{12... | collective-permute-start | bytes 700424 | tf_op jit(solution)/shard_map/ppermute | solution.py:27
  58.4 37.9 %copy-start = (bf16[1,32,64,256]{3,1,2,0:T(8,128)(2,1)S(1)}, bf16[1,32,64,256]{3,1,2,0:T(8,128)(2,1)}, u32[]{:S(2)}) copy-start(bf16[1,32,64,256]{3,1,2,0:T(8,128)(2,1)} %get-tuple-element.162) | copy-start | bytes 3145732
  58.5 37.9 %copy-start.1 = (bf16[1,32,64,256]{3,1,2,0:T(8,128)(2,1)S(1)}, bf16[1,32,64,256]{3,1,2,0:T(8,128)(2,1)}, u32[]{:S(2)}) copy-start(bf16[1,32,64,256]{3,1,2,0:T(8,128)(2,1)} %get-tuple-element.163) | copy-start | bytes 3145732
  58.5 37.9 %copy-start.2 = (bf16[1,32,64,256]{3,1,2,0:T(8,128)(2,1)S(1)}, bf16[1,32,64,256]{3,1,2,0:T(8,128)(2,1)}, u32[]{:S(2)}) copy-start(bf16[1,32,64,256]{3,1,2,0:T(8,128)(2,1)} %get-tuple-element.164) | copy-start | bytes 3145732
  59.0 6.1 %collective-permute-start.4 = (f32[3,2,12,32]{3,2,1,0:T(8,128)S(1)}, f32[3,2,12,32]{3,2,1,0:T(8,128)S(1)}, u32[]{:S(2)}, u32[]{:S(2)}) collective-permute-start(f32[3,2,12,32]{3,2,1,0:T(8,128)S(1)} %get-tuple-element.170), channel_id=1, source_target_pairs={{8,0},{16,8},{24,16},{9,1},{17,9},{25,17},{10,2},{18,10},{26,18},{... | collective-permute-start | bytes 27656 | tf_op jit(solution)/shard_map/ppermute | solution.py:14
  60.4 6.3 %collective-permute-start.5 = (f32[3,2,12,32]{3,2,1,0:T(8,128)S(1)}, f32[3,2,12,32]{3,2,1,0:T(8,128)S(1)}, u32[]{:S(2)}, u32[]{:S(2)}) collective-permute-start(f32[3,2,12,32]{3,2,1,0:T(8,128)S(1)} %get-tuple-element.169), channel_id=1, source_target_pairs={{0,8},{8,16},{16,24},{1,9},{9,17},{17,25},{2,10},{10,18},{18,26},{... | collective-permute-start | bytes 27656 | tf_op jit(solution)/shard_map/ppermute | solution.py:14
  66.7 7.5 %collective-permute-start.6 = (f32[3,4,2,32]{3,2,1,0:T(2,128)S(1)}, f32[3,4,2,32]{3,2,1,0:T(2,128)S(1)}, u32[]{:S(2)}, u32[]{:S(2)}) collective-permute-start(f32[3,4,2,32]{3,2,1,0:T(2,128)S(1)} %get-tuple-element.182), channel_id=1, source_target_pairs={{1,0},{2,1},{3,2},{4,3},{5,4},{6,5},{7,6},{9,8},{10,9},{11,10},{12... | collective-permute-start | bytes 9224 | tf_op jit(solution)/shard_map/ppermute | solution.py:14
  68.1 6.8 %collective-permute-start.7 = (f32[3,4,2,32]{3,2,1,0:T(2,128)S(1)}, f32[3,4,2,32]{3,2,1,0:T(2,128)S(1)}, u32[]{:S(2)}, u32[]{:S(2)}) collective-permute-start(f32[3,4,2,32]{3,2,1,0:T(2,128)S(1)} %get-tuple-element.181), channel_id=1, source_target_pairs={{0,1},{1,2},{2,3},{3,4},{4,5},{5,6},{6,7},{8,9},{9,10},{10,11},{11... | collective-permute-start | bytes 9224 | tf_op jit(solution)/shard_map/ppermute | solution.py:14
  74.9 5.8 %collective-permute-start.8 = (f32[3,2,8,32]{3,2,1,0:T(8,128)S(1)}, f32[3,2,8,32]{3,2,1,0:T(8,128)S(1)}, u32[]{:S(2)}, u32[]{:S(2)}) collective-permute-start(f32[3,2,8,32]{3,2,1,0:T(8,128)S(1)} %get-tuple-element.185), channel_id=1, source_target_pairs={{0,8},{8,16},{16,24},{1,9},{9,17},{17,25},{2,10},{10,18},{18,26},{... | collective-permute-start | bytes 18440 | tf_op jit(solution)/shard_map/ppermute | solution.py:25
  79.2 6.7 %collective-permute-start.9 = (f32[3,2,8,32]{3,2,1,0:T(8,128)S(1)}, f32[3,2,8,32]{3,2,1,0:T(8,128)S(1)}, u32[]{:S(2)}, u32[]{:S(2)}) collective-permute-start(f32[3,2,8,32]{3,2,1,0:T(8,128)S(1)} %get-tuple-element.186), channel_id=1, source_target_pairs={{8,0},{16,8},{24,16},{9,1},{17,9},{25,17},{10,2},{18,10},{26,18},{... | collective-permute-start | bytes 18440 | tf_op jit(solution)/shard_map/ppermute | solution.py:27
  85.9 3.8 %collective-permute-start.10 = (f32[3,8,2,32]{3,2,1,0:T(2,128)S(1)}, f32[3,8,2,32]{3,2,1,0:T(2,128)S(1)}, u32[]{:S(2)}, u32[]{:S(2)}) collective-permute-start(f32[3,8,2,32]{3,2,1,0:T(2,128)S(1)} %get-tuple-element.179), channel_id=1, source_target_pairs={{0,1},{1,2},{2,3},{3,4},{4,5},{5,6},{6,7},{8,9},{9,10},{10,11},{11... | collective-permute-start | bytes 18440 | tf_op jit(solution)/shard_map/ppermute | solution.py:25
  88.4 6.0 %collective-permute-start.11 = (f32[3,8,2,32]{3,2,1,0:T(2,128)S(1)}, f32[3,8,2,32]{3,2,1,0:T(2,128)S(1)}, u32[]{:S(2)}, u32[]{:S(2)}) collective-permute-start(f32[3,8,2,32]{3,2,1,0:T(2,128)S(1)} %get-tuple-element.180), channel_id=1, source_target_pairs={{1,0},{2,1},{3,2},{4,3},{5,4},{6,5},{7,6},{9,8},{10,9},{11,10},{12... | collective-permute-start | bytes 18440 | tf_op jit(solution)/shard_map/ppermute | solution.py:27
  108.4 6.9 %collective-permute-start.12 = (f32[3,2,12,32]{3,2,1,0:T(8,128)S(1)}, f32[3,2,12,32]{3,2,1,0:T(8,128)S(1)}, u32[]{:S(2)}, u32[]{:S(2)}) collective-permute-start(f32[3,2,12,32]{3,2,1,0:T(8,128)S(1)} %get-tuple-element.168), channel_id=1, source_target_pairs={{8,0},{16,8},{24,16},{9,1},{17,9},{25,17},{10,2},{18,10},{26,18},{... | collective-permute-start | bytes 27656 | tf_op jit(solution)/shard_map/ppermute | solution.py:14
  109.7 7.2 %collective-permute-start.13 = (f32[3,2,12,32]{3,2,1,0:T(8,128)S(1)}, f32[3,2,12,32]{3,2,1,0:T(8,128)S(1)}, u32[]{:S(2)}, u32[]{:S(2)}) collective-permute-start(f32[3,2,12,32]{3,2,1,0:T(8,128)S(1)} %get-tuple-element.167), channel_id=1, source_target_pairs={{0,8},{8,16},{16,24},{1,9},{9,17},{17,25},{2,10},{10,18},{18,26},{... | collective-permute-start | bytes 27656 | tf_op jit(solution)/shard_map/ppermute | solution.py:14
  116.9 5.6 %collective-permute-start.14 = (f32[3,4,2,32]{3,2,1,0:T(2,128)S(1)}, f32[3,4,2,32]{3,2,1,0:T(2,128)S(1)}, u32[]{:S(2)}, u32[]{:S(2)}) collective-permute-start(f32[3,4,2,32]{3,2,1,0:T(2,128)S(1)} %get-tuple-element.178), channel_id=1, source_target_pairs={{1,0},{2,1},{3,2},{4,3},{5,4},{6,5},{7,6},{9,8},{10,9},{11,10},{12... | collective-permute-start | bytes 9224 | tf_op jit(solution)/shard_map/ppermute | solution.py:14
  118.3 5.1 %collective-permute-start.15 = (f32[3,4,2,32]{3,2,1,0:T(2,128)S(1)}, f32[3,4,2,32]{3,2,1,0:T(2,128)S(1)}, u32[]{:S(2)}, u32[]{:S(2)}) collective-permute-start(f32[3,4,2,32]{3,2,1,0:T(2,128)S(1)} %get-tuple-element.177), channel_id=1, source_target_pairs={{0,1},{1,2},{2,3},{3,4},{4,5},{5,6},{6,7},{8,9},{9,10},{10,11},{11... | collective-permute-start | bytes 9224 | tf_op jit(solution)/shard_map/ppermute | solution.py:14
  154.1 5.3 %collective-permute-start.16 = (f32[3,2,8,32]{3,2,1,0:T(8,128)S(1)}, f32[3,2,8,32]{3,2,1,0:T(8,128)S(1)}, u32[]{:S(2)}, u32[]{:S(2)}) collective-permute-start(f32[3,2,8,32]{3,2,1,0:T(8,128)S(1)} %get-tuple-element.183), channel_id=1, source_target_pairs={{0,8},{8,16},{16,24},{1,9},{9,17},{17,25},{2,10},{10,18},{18,26},{... | collective-permute-start | bytes 18440 | tf_op jit(solution)/shard_map/ppermute | solution.py:25
  158.0 5.7 %collective-permute-start.17 = (f32[3,2,8,32]{3,2,1,0:T(8,128)S(1)}, f32[3,2,8,32]{3,2,1,0:T(8,128)S(1)}, u32[]{:S(2)}, u32[]{:S(2)}) collective-permute-start(f32[3,2,8,32]{3,2,1,0:T(8,128)S(1)} %get-tuple-element.184), channel_id=1, source_target_pairs={{8,0},{16,8},{24,16},{9,1},{17,9},{25,17},{10,2},{18,10},{26,18},{... | collective-permute-start | bytes 18440 | tf_op jit(solution)/shard_map/ppermute | solution.py:27
  163.7 2.8 %collective-permute-start.18 = (f32[3,8,2,32]{3,2,1,0:T(2,128)S(1)}, f32[3,8,2,32]{3,2,1,0:T(2,128)S(1)}, u32[]{:S(2)}, u32[]{:S(2)}) collective-permute-start(f32[3,8,2,32]{3,2,1,0:T(2,128)S(1)} %get-tuple-element.175), channel_id=1, source_target_pairs={{0,1},{1,2},{2,3},{3,4},{4,5},{5,6},{6,7},{8,9},{9,10},{10,11},{11... | collective-permute-start | bytes 18440 | tf_op jit(solution)/shard_map/ppermute | solution.py:25
  165.0 3.1 %collective-permute-start.19 = (f32[3,8,2,32]{3,2,1,0:T(2,128)S(1)}, f32[3,8,2,32]{3,2,1,0:T(2,128)S(1)}, u32[]{:S(2)}, u32[]{:S(2)}) collective-permute-start(f32[3,8,2,32]{3,2,1,0:T(2,128)S(1)} %get-tuple-element.176), channel_id=1, source_target_pairs={{1,0},{2,1},{3,2},{4,3},{5,4},{6,5},{7,6},{9,8},{10,9},{11,10},{12... | collective-permute-start | bytes 18440 | tf_op jit(solution)/shard_map/ppermute | solution.py:27
  182.1 6.4 %collective-permute-start.20 = (f32[3,2,12,32]{3,2,1,0:T(8,128)S(1)}, f32[3,2,12,32]{3,2,1,0:T(8,128)S(1)}, u32[]{:S(2)}, u32[]{:S(2)}) collective-permute-start(f32[3,2,12,32]{3,2,1,0:T(8,128)S(1)} %get-tuple-element.166), channel_id=1, source_target_pairs={{8,0},{16,8},{24,16},{9,1},{17,9},{25,17},{10,2},{18,10},{26,18},{... | collective-permute-start | bytes 27656 | tf_op jit(solution)/shard_map/ppermute | solution.py:14
  183.4 6.3 %collective-permute-start.21 = (f32[3,2,12,32]{3,2,1,0:T(8,128)S(1)}, f32[3,2,12,32]{3,2,1,0:T(8,128)S(1)}, u32[]{:S(2)}, u32[]{:S(2)}) collective-permute-start(f32[3,2,12,32]{3,2,1,0:T(8,128)S(1)} %get-tuple-element.165), channel_id=1, source_target_pairs={{0,8},{8,16},{16,24},{1,9},{9,17},{17,25},{2,10},{10,18},{18,26},{... | collective-permute-start | bytes 27656 | tf_op jit(solution)/shard_map/ppermute | solution.py:14
  189.7 4.4 %collective-permute-start.22 = (f32[3,4,2,32]{3,2,1,0:T(2,128)S(1)}, f32[3,4,2,32]{3,2,1,0:T(2,128)S(1)}, u32[]{:S(2)}, u32[]{:S(2)}) collective-permute-start(f32[3,4,2,32]{3,2,1,0:T(2,128)S(1)} %get-tuple-element.174), channel_id=1, source_target_pairs={{1,0},{2,1},{3,2},{4,3},{5,4},{6,5},{7,6},{9,8},{10,9},{11,10},{12... | collective-permute-start | bytes 9224 | tf_op jit(solution)/shard_map/ppermute | solution.py:14
  191.0 3.9 %collective-permute-start.23 = (f32[3,4,2,32]{3,2,1,0:T(2,128)S(1)}, f32[3,4,2,32]{3,2,1,0:T(2,128)S(1)}, u32[]{:S(2)}, u32[]{:S(2)}) collective-permute-start(f32[3,4,2,32]{3,2,1,0:T(2,128)S(1)} %get-tuple-element.173), channel_id=1, source_target_pairs={{0,1},{1,2},{2,3},{3,4},{4,5},{5,6},{6,7},{8,9},{9,10},{10,11},{11... | collective-permute-start | bytes 9224 | tf_op jit(solution)/shard_map/ppermute | solution.py:14
